TPU v7x, 32 devices: a whole 2x2x4 slice. The times are simulated.
32 devices in a mesh: grp: 4 (over y, core), ch: 8 (over z, x).
Axes of the slice: x: 2, y: 2, z: 4, core: 2. Of those that a mesh axis runs over, the one named last changes fastest.
Arguments:
- strain: bfloat16 [8, 1024, 4096], P('grp', 'ch'), may hold values from -6 to 6
- valid_mask: int32 [8, 1024], P('grp', 'ch'), may hold values 0 or 1
- pair_list: int32 [8, 6, 2], P('ch'), may hold values from 0 to 7, as said below
- owner_group: int32 [8, 6], P('ch'), may hold values from 0 to 3, as said below
Outputs:
- stacks: float32 [4, 8, 2, 128, 4096], P('grp', 'ch')
Inputs may be any that keep to these rules, and one draw needn't show every extreme that they name: `pair_list`: entries are channel block numbers; each ordered pair of blocks appears at most once over all columns. `owner_group`: in each column no group owns more than 2 entries, and some group owns exactly 2.
All inputs are finite; a program needn't handle non-finite values. No bound on the sum of `valid_mask` on one device may be relied on, other than what follows from the above.
Results may differ from a plain program's by a relative error of at most 0.0042.
Values may be sent and summed in bfloat16 or wider, within the bound.
A program may use at most 192 MiB of HBM per device.

v0:
```python
import math
import jax
import jax.numpy as jnp
from jax import lax
from jax.sharding import PartitionSpec as P

NFFT = 4096
NB = 1024
SUB = 64
BLK = 128
CAP = 2


def forward_table(length, bins):
    samples = jnp.arange(length, dtype=jnp.int32)
    frequency = jnp.arange(1, bins + 1, dtype=jnp.int32)
    angles = jnp.mod(samples[:, None] * frequency[None, :], length).astype(jnp.float32) * (
        2.0 * math.pi / length
    )
    hann_taper = 0.5 - 0.5 * jnp.cos(samples.astype(jnp.float32) * (2.0 * math.pi / length))
    return jnp.concatenate(
        [hann_taper[:, None] * jnp.cos(angles), -hann_taper[:, None] * jnp.sin(angles)], axis=1
    ).astype(jnp.bfloat16)


def inverse_table(length, bins):
    frequency = jnp.arange(1, bins + 1, dtype=jnp.int32)
    lag_index = jnp.arange(length, dtype=jnp.int32) - length // 2
    angles = jnp.mod(frequency[:, None] * lag_index[None, :], length).astype(jnp.float32) * (
        2.0 * math.pi / length
    )
    return jnp.concatenate([jnp.cos(angles), -jnp.sin(angles)], axis=0)


def whiten_rows(spectrum, valid_mask, bins, band):
    real_part = spectrum[..., :bins]
    imag_part = spectrum[..., bins:]
    power = real_part * real_part + imag_part * imag_part
    band_power = jnp.sum(power.reshape(power.shape[:-1] + (bins // band, band)), axis=-1) / band
    norm_full = jnp.repeat(jnp.sqrt(band_power + 1e-06), band, axis=-1)
    norm_both = jnp.concatenate([norm_full, norm_full], axis=-1)
    return (spectrum / norm_both * valid_mask[..., None].astype(jnp.float32)).astype(jnp.bfloat16)


def cross_block(rows, pair_entry, block, bins):
    first_rows = lax.dynamic_slice_in_dim(rows, pair_entry[0] * block, block, 1).astype(jnp.float32)
    second_rows = lax.dynamic_slice_in_dim(rows, pair_entry[1] * block, block, 1).astype(
        jnp.float32
    )
    first_real = first_rows[..., :bins]
    first_imag = first_rows[..., bins:]
    second_real = second_rows[..., :bins]
    second_imag = second_rows[..., bins:]
    cross_real = jnp.sum(first_real * second_real + first_imag * second_imag, axis=0)
    cross_imag = jnp.sum(first_real * second_imag - first_imag * second_real, axis=0)
    return jnp.concatenate([cross_real, cross_imag], axis=-1)


def local(strain, valid_mask, pair_list, owner_group):
    window_count = strain.shape[0]
    groups = lax.axis_size("grp")
    forward = forward_table(NFFT, NB)
    spectrum = jnp.dot(strain.reshape(-1, NFFT), forward, preferred_element_type=jnp.float32)
    spectrum = spectrum.reshape(strain.shape[0], strain.shape[1], 2 * NB)
    white = whiten_rows(spectrum, valid_mask, NB, SUB)
    gathered = lax.all_gather(white, "ch", axis=1, tiled=True)
    pair_codes = pair_list[0]
    partial_value = lax.map(
        lambda pair_entry: cross_block(gathered, pair_entry, BLK, NB), pair_codes
    )
    owners = owner_group[0]
    list_len = owners.shape[0]
    positions = jnp.arange(list_len, dtype=jnp.int32)
    earlier = positions[None, :] < positions[:, None]
    slot_rank = jnp.sum(((owners[:, None] == owners[None, :]) & earlier).astype(jnp.int32), axis=1)
    slot_ids = jnp.arange(CAP, dtype=jnp.int32)
    flat_partial = partial_value.reshape(list_len, -1)
    summed = lax.psum(flat_partial, "grp")
    my_group = lax.axis_index("grp")
    picking = ((owners[None, :] == my_group) & (slot_rank[None, :] == slot_ids[:, None])).astype(
        jnp.float32
    )
    total = jnp.dot(
        picking, summed, precision=lax.Precision.HIGHEST, preferred_element_type=jnp.float32
    )
    inverse = inverse_table(NFFT, NB)
    stacked = jnp.dot(
        total.reshape(-1, 2 * NB),
        inverse,
        precision=lax.Precision.HIGHEST,
        preferred_element_type=jnp.float32,
    )
    scale = 1.0 / math.sqrt(NB * window_count * groups)
    return (stacked * scale).reshape(1, 1, CAP, BLK, NFFT)


def solution(mesh):
    placed = (P("grp", "ch", None), P("grp", "ch"), P("ch", None, None), P("ch", None))
    return jax.shard_map(
        local,
        mesh=mesh,
        in_specs=placed,
        out_specs=P("grp", "ch", None, None, None),
        check_vma=False,
    )
```

profile of v0, /device:TPU:0, one launch (start us, length us, event | category | flops | bytes accessed | tf_op | source)
XLA Modules:
  0.0 475.3 jit_solution(4424673960620839761)
XLA Ops:
  7.4 69.9 %multiply_convert_fusion.1 = (bf16[4096,1024]{1,0:T(8,128)(2,1)}, bf16[4096,1024]{1,0:T(8,128)(2,1)}) fusion(s32[1024]{0:T(1024)S(1)} %iota_add_fusion.1, f32[4096]{0:T(1024)S(1)} %get-tuple-element.54, f32[4096]{0:T(1024)S(1)} %get-tuple-element.55), kind=kLoop, calls=%fused_computation.31 | loop fusion | flops 75497472 | bytes 16814080 | tf_op jit(solution)/shard_map/convert
  77.4 9.8 %fusion.11 = f32[2048,256]{0,1:T(8,128)} fusion(bf16[256,4096]{1,0:T(8,128)(2,1)S(1)} %bitcast.29, bf16[4096,1024]{1,0:T(8,128)(2,1)} %get-tuple-element.53, bf16[4096,1024]{1,0:T(8,128)(2,1)} %get-tuple-element.52), kind=kOutput, calls=%fused_computation.25 | convolution fusion | flops 4328521728 | bytes 20971520 | tf_op jit(solution)/shard_map/dot_general | solution.py:63
  87.2 1.9 copy.11
  89.5 1.2 fusion.23
  91.0 127.6 %all-gather.2.cloned.1.call-done = bf16[2,1024,2048]{1,2,0:T(8,128)(2,1)} async-done(((bf16[2,128,2048]{1,2,0:T(8,128)(2,1)}), bf16[2,1024,2048]{1,2,0:T(8,128)(2,1)}) %all-gather.2.cloned.1.call-update) | async-done | bytes 8388624 | tf_op jit(solution)/shard_map/all_gather | solution.py:66
  218.5 11.7 %copy.12 = bf16[2,1024,2048]{2,1,0:T(8,128)(2,1)} copy(bf16[2,1024,2048]{1,2,0:T(8,128)(2,1)} %all-gather.2.cloned.1.call-done) | data formatting | bytes 16777216 | tf_op jit(solution)/shard_map/while | solution.py:68
  230.2 32.5 %while.10 = (s32[]{:T(128)}, f32[6,128,2048]{2,1,0:T(8,128)}, s32[6,2]{0,1:T(2,128)S(1)}, bf16[2,1024,2048]{2,1,0:T(8,128)(2,1)}, s32[]{:T(128)}, /*index=5*/s32[1,1]{0,1:T(1,128)}, s32[]{:T(128)}, s32[]{:T(128)}) while((s32[]{:T(128)}, f32[6,128,2048]{2,1,0:T(8,128)}, s32[6,2]{0,1:T(2,128)S(1)}, bf16[2,1024,2048]{2,1,0:T(8,128)(2,1)}, ...), condition=%wide.region_5.6_spmd, body=%wide.region_2.0_spmd.sunk | while | flops 3145738 | bytes 13631721 | solution.py:68
  232.1 1.9 dynamic-slice_convert_fusion.3
  234.6 1.1 fusion.42
  237.5 1.9 dynamic-slice_convert_fusion.3
  240.0 1.1 fusion.42
  242.9 1.9 dynamic-slice_convert_fusion.3
  245.4 1.1 fusion.42
  248.4 1.9 dynamic-slice_convert_fusion.3
  253.8 1.9 dynamic-slice_convert_fusion.3
  256.2 1.1 fusion.42
  259.2 1.9 dynamic-slice_convert_fusion.3
  261.6 1.1 fusion.42
  262.7 9.8 %copy.13 = f32[1,6,128,2048]{3,1,2,0:T(8,128)} copy(f32[1,6,128,2048]{3,2,1,0:T(8,128)} %bitcast.31) | data formatting | bytes 12582912
  272.7 68.4 %fusion.18 = (f32[1024,4096]{1,0:T(8,128)}, f32[1024,4096]{1,0:T(8,128)}) fusion(s32[4096]{0:T(1024)S(1)} %iota_add_fusion, s32[1024]{0:T(1024)S(1)} %iota_add_fusion.1), kind=kLoop, calls=%fused_computation.35 | loop fusion | flops 62914560 | bytes 33574912 | tf_op jit(solution)/shard_map/cos | solution.py:32
  341.2 82.5 %all-reduce.2.cloned.1.call-done = f32[6,262144]{1,0:T(8,128)} async-done(((f32[6,262144]{1,0:T(8,128)}), f32[6,262144]{1,0:T(8,128)}) %all-reduce.2.cloned.1.call-update) | async-done | bytes 6291472 | tf_op jit(solution)/shard_map/psum | solution.py:78
  423.7 7.4 %fusion.27 = f32[2,262144]{1,0:T(2,128)S(1)} fusion(f32[6,262144]{1,0:T(8,128)} %all-reduce.2.cloned.1.call-done, pred[6]{0:T(512)(128)(4,1)S(1)} %compare_bitcast_fusion, s32[6]{0:T(128)S(1)} %convert_reduce_fusion), kind=kOutput, calls=%fused_computation.52 | convolution fusion | flops 37748760 | bytes 8388638 | tf_op jit(solution)/shard_map/dot_general | solution.py:83
  431.1 3.1 reshape.62
  434.2 34.3 %fusion.19 = f32[256,4096]{1,0:T(8,128)} fusion(f32[256,2048]{1,0:T(8,128)} %reshape.62, f32[1024,4096]{1,0:T(8,128)} %get-tuple-element.51, f32[1024,4096]{1,0:T(8,128)} %get-tuple-element.50), kind=kOutput, calls=%fused_computation.36 | convolution fusion | flops 25779240960 | bytes 39845888 | tf_op jit(solution)/shard_map/dot_general | solution.py:87
  (41 shorter events, 9.7 us)
Async XLA Ops:
  6.5 70.9 %copy-start = (bf16[2,128,4096]{2,1,0:T(8,128)(2,1)S(1)}, bf16[2,128,4096]{2,1,0:T(8,128)(2,1)}, u32[]{:S(2)}) copy-start(bf16[2,128,4096]{2,1,0:T(8,128)(2,1)} %param.6) | copy-start | bytes 6291460
  6.5 212.0 %all-gather.2.cloned.1.call-start = ((), (), s32[]{:S(2)}) async-start(), calls=%async_computation | async-start | bytes 9437184 | tf_op jit(solution)/shard_map/all_gather | solution.py:66
  90.7 333.0 %all-reduce.2.cloned.1.call-start = ((), (), s32[]{:S(2)}) async-start(), calls=%async_computation.1 | async-start | bytes 16777216 | tf_op jit(solution)/shard_map/psum | solution.py:78
  91.0 139.3 %copy-start.2 = (s32[1,6,2]{1,2,0:T(2,128)S(1)}, s32[1,6,2]{1,2,0:T(2,128)}, u32[]{:S(2)}) copy-start(s32[1,6,2]{1,2,0:T(2,128)} %param.8) | copy-start | bytes 148
  262.7 9.8 %copy-start.3 = (s32[1,6]{1,0:T(1,128)S(1)}, s32[1,6]{1,0:T(1,128)}, u32[]{:S(2)}) copy-start(s32[1,6]{1,0:T(1,128)} %param.9) | copy-start | bytes 76
  434.2 34.3 %copy-start.1 = (bf16[2,128,4096]{2,1,0:T(8,128)(2,1)S(1)}, bf16[2,128,4096]{2,1,0:T(8,128)(2,1)}, u32[]{:S(2)}) copy-start(bf16[2,128,4096]{2,1,0:T(8,128)(2,1)} %param.6) | copy-start | bytes 6291460
Sparse Core Ops, SparseCore 0:
  90.9 127.6 all-gather.1
  272.6 151.0 all-reduce.1
where the time goes:
time: 476 us; the launch traced here: 475 us
  waiting for transfers between devices  210 us (44%)
  other arithmetic  162 us (34%)
  matrix products  51.5 us (11%)
  local copies, waits for them, and re-layouts  30.2 us (6%)
  between operations  13.5 us (3%)
  loops' own time  7.78 us (2%)
    all_gather x1, waiting for transfers between devices, local(): gathered = lax.all_gather(white, 'ch', axis=1, tiled=True)  128 us
    psum x1, waiting for transfers between devices, local(): summed = lax.psum(flat_partial, 'grp')  82.5 us
    another operation x1, other arithmetic  69.9 us
    cos x1, other arithmetic, inverse_table(): return jnp.concatenate([jnp.cos(angles), -jnp.sin(angles)], axis=0)  68.4 us
    dot_general x1, matrix products, local(): jnp.dot(total.reshape(-1, 2 * NB), inverse, precision=lax.Precision.HIGHE...  34.3 us
    while x1, local copies, waits for them, and re-layouts, local(): lax.map(lambda pair_entry: cross_block(gathered, pair_entry, BLK, NB), pa...  11.7 us
    convert_element_type x6, other arithmetic, cross_block(): lax.dynamic_slice_in_dim(rows, pair_entry[0] * block, block, 1)  11.3 us
    dot_general x1, matrix products, local(): jnp.dot(strain.reshape(-1, NFFT), forward, preferred_element_type=jnp.flo...  9.8 us
  transfers between devices with their start and end apart: 2, of which 2 were waited for; matrix products, arithmetic and copies ran while one was open for 14% of the time, Pallas kernels for 0%

commit v1 on v0

--- a/solution.py
+++ b/solution.py
@@ -63,7 +63,12 @@
     spectrum = jnp.dot(strain.reshape(-1, NFFT), forward, preferred_element_type=jnp.float32)
     spectrum = spectrum.reshape(strain.shape[0], strain.shape[1], 2 * NB)
     white = whiten_rows(spectrum, valid_mask, NB, SUB)
-    gathered = lax.all_gather(white, "ch", axis=1, tiled=True)
+    ring = [white]
+    for hop in range(7):
+        ring.append(lax.ppermute(ring[-1], "ch", [(dev, (dev + 1) % 8) for dev in range(8)]))
+    gathered = jnp.roll(
+        jnp.concatenate(ring[::-1], axis=1), (lax.axis_index("ch") + 1) * ring[0].shape[1], axis=1
+    )
     pair_codes = pair_list[0]
     partial_value = lax.map(
         lambda pair_entry: cross_block(gathered, pair_entry, BLK, NB), pair_codes

time: 476 us -> 563 us (1.18)
  waiting for transfers between devices: 210 us -> 256 us
  local copies, waits for them, and re-layouts: 30.2 us -> 67.6 us
    ppermute x0 -> x7, waiting for transfers between devices: none -> 176 us  [local(): lax.ppermute(ring[-1], 'ch', [(dev, (dev + 1) % 8) for dev in range(8)])]
    all_gather x1 -> x0, waiting for transfers between devices: 128 us -> none  [local(): gathered = lax.all_gather(white, 'ch', axis=1, tiled=True)]
    unnamed x9 -> x38, local copies, waits for them, and re-layouts: 9.79 us -> 38.2 us
    dynamic_slice x0 -> x1, local copies, waits for them, and re-layouts: none -> 7.6 us  [local(): jnp.roll(jnp.concatenate(ring[::-1], axis=1), (lax.axis_index('ch') + 1)...]
  transfers between devices with their start and end apart: 2 -> 8, of which waited for: 2 -> 8; matrix products, arithmetic and copies ran while one was open for 14% -> 12% of each run, Pallas kernels for 0% -> 0%
where the time goes in v1:
time: 563 us; the launch traced here: 562 us
  waiting for transfers between devices  256 us (45%)
  other arithmetic  162 us (29%)
  local copies, waits for them, and re-layouts  67.6 us (12%)
  matrix products  51.5 us (9%)
  between operations  13.5 us (2%)
  loops' own time  7.79 us (1%)
    ppermute x7, waiting for transfers between devices, local(): lax.ppermute(ring[-1], 'ch', [(dev, (dev + 1) % 8) for dev in range(8)])  176 us
    psum x1, waiting for transfers between devices, local(): summed = lax.psum(flat_partial, 'grp')  80.5 us
    another operation x1, other arithmetic  70 us
    cos x1, other arithmetic, inverse_table(): return jnp.concatenate([jnp.cos(angles), -jnp.sin(angles)], axis=0)  68.4 us
    unnamed x38, local copies, waits for them, and re-layouts  38.2 us
    dot_general x1, matrix products, local(): jnp.dot(total.reshape(-1, 2 * NB), inverse, precision=lax.Precision.HIGHE...  34.2 us
    convert_element_type x6, other arithmetic, cross_block(): lax.dynamic_slice_in_dim(rows, pair_entry[0] * block, block, 1)  12.4 us
    while x1, local copies, waits for them, and re-layouts, local(): lax.map(lambda pair_entry: cross_block(gathered, pair_entry, BLK, NB), pa...  11.7 us
  transfers between devices with their start and end apart: 8, of which 8 were waited for; matrix products, arithmetic and copies ran while one was open for 12% of the time, Pallas kernels for 0%

profile of v1, /device:TPU:0, one launch (start us, length us, event | category | flops | bytes accessed | tf_op | source)
XLA Modules:
  0.0 561.6 jit_solution(5710102013157547280)
XLA Ops:
  6.6 70.0 %multiply_convert_fusion.1 = (bf16[4096,1024]{1,0:T(8,128)(2,1)}, bf16[4096,1024]{1,0:T(8,128)(2,1)}) fusion(s32[1024]{0:T(1024)S(1)} %iota_add_fusion.1, f32[4096]{0:T(1024)S(1)} %get-tuple-element.54, f32[4096]{0:T(1024)S(1)} %get-tuple-element.55), kind=kLoop, calls=%fused_computation.31 | loop fusion | flops 75497472 | bytes 16814080 | tf_op jit(solution)/shard_map/convert
  76.7 9.8 %fusion.11 = f32[2048,256]{0,1:T(8,128)} fusion(bf16[256,4096]{1,0:T(8,128)(2,1)S(1)} %bitcast.29, bf16[4096,1024]{1,0:T(8,128)(2,1)} %get-tuple-element.53, bf16[4096,1024]{1,0:T(8,128)(2,1)} %get-tuple-element.52), kind=kOutput, calls=%fused_computation.25 | convolution fusion | flops 4328521728 | bytes 20971520 | tf_op jit(solution)/shard_map/dot_general | solution.py:63
  89.0 3.0 collective-permute-start
  92.1 26.2 %collective-permute-done = bf16[2,128,2048]{1,2,0:T(8,128)(2,1)S(1)} collective-permute-done((bf16[2,128,2048]{1,2,0:T(8,128)(2,1)S(1)}, bf16[2,128,2048]{1,2,0:T(8,128)(2,1)S(1)}, u32[]{:S(2)}, u32[]{:S(2)}) %collective-permute-start) | collective-permute-done | bytes 1048608 | tf_op jit(solution)/shard_map/ppermute | solution.py:68
  118.3 27.0 %collective-permute-done.1 = bf16[2,128,2048]{1,2,0:T(8,128)(2,1)S(1)} collective-permute-done((bf16[2,128,2048]{1,2,0:T(8,128)(2,1)S(1)}, bf16[2,128,2048]{1,2,0:T(8,128)(2,1)S(1)}, u32[]{:S(2)}, u32[]{:S(2)}) %collective-permute-start.1) | collective-permute-done | bytes 1048608 | tf_op jit(solution)/shard_map/ppermute | solution.py:68
  145.3 26.2 %collective-permute-done.2 = bf16[2,128,2048]{1,2,0:T(8,128)(2,1)S(1)} collective-permute-done((bf16[2,128,2048]{1,2,0:T(8,128)(2,1)S(1)}, bf16[2,128,2048]{1,2,0:T(8,128)(2,1)S(1)}, u32[]{:S(2)}, u32[]{:S(2)}) %collective-permute-start.2) | collective-permute-done | bytes 1048608 | tf_op jit(solution)/shard_map/ppermute | solution.py:68
  172.4 25.3 %collective-permute-done.3 = bf16[2,128,2048]{1,2,0:T(8,128)(2,1)S(1)} collective-permute-done((bf16[2,128,2048]{1,2,0:T(8,128)(2,1)S(1)}, bf16[2,128,2048]{1,2,0:T(8,128)(2,1)S(1)}, u32[]{:S(2)}, u32[]{:S(2)}) %collective-permute-start.3) | collective-permute-done | bytes 1048608 | tf_op jit(solution)/shard_map/ppermute | solution.py:68
  198.7 24.4 %collective-permute-done.4 = bf16[2,128,2048]{1,2,0:T(8,128)(2,1)S(1)} collective-permute-done((bf16[2,128,2048]{1,2,0:T(8,128)(2,1)S(1)}, bf16[2,128,2048]{1,2,0:T(8,128)(2,1)S(1)}, u32[]{:S(2)}, u32[]{:S(2)}) %collective-permute-start.4) | collective-permute-done | bytes 1048608 | tf_op jit(solution)/shard_map/ppermute | solution.py:68
  224.2 23.7 %collective-permute-done.5 = bf16[2,128,2048]{1,2,0:T(8,128)(2,1)} collective-permute-done((bf16[2,128,2048]{1,2,0:T(8,128)(2,1)S(1)}, bf16[2,128,2048]{1,2,0:T(8,128)(2,1)}, u32[]{:S(2)}, u32[]{:S(2)}) %collective-permute-start.5) | collective-permute-done | bytes 1048608 | tf_op jit(solution)/shard_map/ppermute | solution.py:68
  247.9 23.0 %collective-permute-done.6 = bf16[2,128,2048]{1,2,0:T(8,128)(2,1)} collective-permute-done((bf16[2,128,2048]{1,2,0:T(8,128)(2,1)}, bf16[2,128,2048]{1,2,0:T(8,128)(2,1)}, u32[]{:S(2)}, u32[]{:S(2)}) %collective-permute-start.6) | collective-permute-done | bytes 1048608 | tf_op jit(solution)/shard_map/ppermute | solution.py:68
  270.9 2.3 constant_dynamic-update-slice_fusion.15
  273.3 2.4 constant_dynamic-update-slice_fusion.14
  275.6 2.4 constant_dynamic-update-slice_fusion.13
  280.3 2.4 constant_dynamic-update-slice_fusion.11
  288.4 2.4 constant_dynamic-update-slice_fusion.6
  297.5 7.6 %constant_dynamic-slice_fusion.1 = bf16[2,1024,2048]{1,2,0:T(8,128)(2,1)} fusion(bf16[2,2048,2048]{1,2,0:T(8,128)(2,1)} %constant_dynamic-update-slice_fusion, s32[]{:T(128)S(6)} %select_n.37), kind=kLoop, calls=%fused_computation.75 | loop fusion | bytes 16777220 | tf_op jit(solution)/shard_map/jit(_roll_dynamic)/dynamic_slice | solution.py:69
  305.1 11.7 %copy.12 = bf16[2,1024,2048]{2,1,0:T(8,128)(2,1)} copy(bf16[2,1024,2048]{1,2,0:T(8,128)(2,1)} %constant_dynamic-slice_fusion.1) | data formatting | bytes 16777216 | tf_op jit(solution)/shard_map/while | solution.py:73
  316.7 34.2 %while.10 = (s32[]{:T(128)}, f32[6,128,2048]{2,1,0:T(8,128)}, s32[6,2]{0,1:T(2,128)S(1)}, bf16[2,1024,2048]{2,1,0:T(8,128)(2,1)}, s32[]{:T(128)}, /*index=5*/s32[1,1]{0,1:T(1,128)}, s32[]{:T(128)}, s32[]{:T(128)}) while((s32[]{:T(128)}, f32[6,128,2048]{2,1,0:T(8,128)}, s32[6,2]{0,1:T(2,128)S(1)}, bf16[2,1024,2048]{2,1,0:T(8,128)(2,1)}, ...), condition=%wide.region_5.6_spmd, body=%wide.region_2.5_spmd.sunk | while | flops 3145738 | bytes 13632221 | solution.py:73
  351.0 9.8 %copy.13 = f32[1,6,128,2048]{3,1,2,0:T(8,128)} copy(f32[1,6,128,2048]{3,2,1,0:T(8,128)} %bitcast.31) | data formatting | bytes 12582912
  361.0 68.4 %fusion.18 = (f32[1024,4096]{1,0:T(8,128)}, f32[1024,4096]{1,0:T(8,128)}) fusion(s32[4096]{0:T(1024)S(1)} %iota_add_fusion, s32[1024]{0:T(1024)S(1)} %iota_add_fusion.1), kind=kLoop, calls=%fused_computation.35 | loop fusion | flops 62914560 | bytes 33574912 | tf_op jit(solution)/shard_map/cos | solution.py:32
  429.4 80.5 %all-reduce.2.cloned.1.call-done = f32[6,262144]{1,0:T(8,128)} async-done(((f32[6,262144]{1,0:T(8,128)}), f32[6,262144]{1,0:T(8,128)}) %all-reduce.2.cloned.1.call-update) | async-done | bytes 6291472 | tf_op jit(solution)/shard_map/psum | solution.py:83
  509.9 7.4 %fusion.27 = f32[2,262144]{1,0:T(2,128)S(1)} fusion(f32[6,262144]{1,0:T(8,128)} %all-reduce.2.cloned.1.call-done, pred[6]{0:T(512)(128)(4,1)S(1)} %compare_bitcast_fusion, s32[6]{0:T(128)S(1)} %convert_reduce_fusion), kind=kOutput, calls=%fused_computation.68 | convolution fusion | flops 37748760 | bytes 8388638 | tf_op jit(solution)/shard_map/dot_general | solution.py:88
  517.3 3.1 reshape.62
  520.5 34.2 %fusion.19 = f32[256,4096]{1,0:T(8,128)} fusion(f32[256,2048]{1,0:T(8,128)} %reshape.62, f32[1024,4096]{1,0:T(8,128)} %get-tuple-element.51, f32[1024,4096]{1,0:T(8,128)} %get-tuple-element.50), kind=kOutput, calls=%fused_computation.36 | convolution fusion | flops 25779240960 | bytes 39845888 | tf_op jit(solution)/shard_map/dot_general | solution.py:92
  (83 shorter events, 46.9 us)
Async XLA Ops:
  6.5 70.1 %copy-start = (bf16[2,128,4096]{2,1,0:T(8,128)(2,1)S(1)}, bf16[2,128,4096]{2,1,0:T(8,128)(2,1)}, u32[]{:S(2)}) copy-start(bf16[2,128,4096]{2,1,0:T(8,128)(2,1)} %param.6) | copy-start | bytes 6291460
  6.5 503.4 %all-reduce.2.cloned.1.call-start = ((), (), s32[]{:S(2)}) async-start(), calls=%async_computation | async-start | bytes 16777216 | tf_op jit(solution)/shard_map/psum | solution.py:83
  76.7 12.0 %copy-start.9 = (s32[2,128]{1,0:T(2,128)S(1)}, s32[2,128]{1,0:T(2,128)}, u32[]{:S(2)}) copy-start(s32[2,128]{1,0:T(2,128)} %param.7) | copy-start | bytes 3076
  89.0 29.2 %collective-permute-start = (bf16[2,128,2048]{1,2,0:T(8,128)(2,1)S(1)}, bf16[2,128,2048]{1,2,0:T(8,128)(2,1)S(1)}, u32[]{:S(2)}, u32[]{:S(2)}) collective-permute-start(bf16[2,128,2048]{1,2,0:T(8,128)(2,1)S(1)} %fusion.23), channel_id=1, source_target_pairs={{0,1},{1,2},{2,3},{3,4},{4,5},{5,6},{6,7},{7,0},{8,9},{9,10},{10,1... | collective-permute-start | bytes 3145736 | tf_op jit(solution)/shard_map/ppermute | solution.py:68
  118.3 27.0 %collective-permute-start.1 = (bf16[2,128,2048]{1,2,0:T(8,128)(2,1)S(1)}, bf16[2,128,2048]{1,2,0:T(8,128)(2,1)S(1)}, u32[]{:S(2)}, u32[]{:S(2)}) collective-permute-start(bf16[2,128,2048]{1,2,0:T(8,128)(2,1)S(1)} %collective-permute-done), channel_id=1, source_target_pairs={{0,1},{1,2},{2,3},{3,4},{4,5},{5,6},{6,7},{7,0},{8,9},{9,10},{10,1... | collective-permute-start | bytes 3145736 | tf_op jit(solution)/shard_map/ppermute | solution.py:68
  145.3 26.2 %collective-permute-start.2 = (bf16[2,128,2048]{1,2,0:T(8,128)(2,1)S(1)}, bf16[2,128,2048]{1,2,0:T(8,128)(2,1)S(1)}, u32[]{:S(2)}, u32[]{:S(2)}) collective-permute-start(bf16[2,128,2048]{1,2,0:T(8,128)(2,1)S(1)} %collective-permute-done.1), channel_id=1, source_target_pairs={{0,1},{1,2},{2,3},{3,4},{4,5},{5,6},{6,7},{7,0},{8,9},{9,10},{10,1... | collective-permute-start | bytes 3145736 | tf_op jit(solution)/shard_map/ppermute | solution.py:68
  171.4 1.0 copy-start.2
  172.4 25.3 %collective-permute-start.3 = (bf16[2,128,2048]{1,2,0:T(8,128)(2,1)S(1)}, bf16[2,128,2048]{1,2,0:T(8,128)(2,1)S(1)}, u32[]{:S(2)}, u32[]{:S(2)}) collective-permute-start(bf16[2,128,2048]{1,2,0:T(8,128)(2,1)S(1)} %collective-permute-done.2), channel_id=1, source_target_pairs={{0,1},{1,2},{2,3},{3,4},{4,5},{5,6},{6,7},{7,0},{8,9},{9,10},{10,1... | collective-permute-start | bytes 3145736 | tf_op jit(solution)/shard_map/ppermute | solution.py:68
  197.7 1.0 copy-start.4
  198.7 24.5 %collective-permute-start.4 = (bf16[2,128,2048]{1,2,0:T(8,128)(2,1)S(1)}, bf16[2,128,2048]{1,2,0:T(8,128)(2,1)S(1)}, u32[]{:S(2)}, u32[]{:S(2)}) collective-permute-start(bf16[2,128,2048]{1,2,0:T(8,128)(2,1)S(1)} %collective-permute-done.3), channel_id=1, source_target_pairs={{0,1},{1,2},{2,3},{3,4},{4,5},{5,6},{6,7},{7,0},{8,9},{9,10},{10,1... | collective-permute-start | bytes 3145736 | tf_op jit(solution)/shard_map/ppermute | solution.py:68
  223.2 1.0 copy-start.6
  224.2 23.7 %collective-permute-start.5 = (bf16[2,128,2048]{1,2,0:T(8,128)(2,1)S(1)}, bf16[2,128,2048]{1,2,0:T(8,128)(2,1)}, u32[]{:S(2)}, u32[]{:S(2)}) collective-permute-start(bf16[2,128,2048]{1,2,0:T(8,128)(2,1)S(1)} %collective-permute-done.4), channel_id=1, source_target_pairs={{0,1},{1,2},{2,3},{3,4},{4,5},{5,6},{6,7},{7,0},{8,9},{9,10},{10,1... | collective-permute-start | bytes 3145736 | tf_op jit(solution)/shard_map/ppermute | solution.py:68
  247.9 23.1 %collective-permute-start.6 = (bf16[2,128,2048]{1,2,0:T(8,128)(2,1)}, bf16[2,128,2048]{1,2,0:T(8,128)(2,1)}, u32[]{:S(2)}, u32[]{:S(2)}) collective-permute-start(bf16[2,128,2048]{1,2,0:T(8,128)(2,1)} %collective-permute-done.5), channel_id=1, source_target_pairs={{0,1},{1,2},{2,3},{3,4},{4,5},{5,6},{6,7},{7,0},{8,9},{9,10},{10,1... | collective-permute-start | bytes 3145736 | tf_op jit(solution)/shard_map/ppermute | solution.py:68
  247.9 42.9 %copy-start.7 = (bf16[2,128,2048]{1,2,0:T(8,128)(2,1)S(1)}, bf16[2,128,2048]{1,2,0:T(8,128)(2,1)}, u32[]{:S(2)}) copy-start(bf16[2,128,2048]{1,2,0:T(8,128)(2,1)} %copy-done.6) | copy-start | bytes 3145732
  247.9 44.1 %copy-start.5 = (bf16[2,128,2048]{1,2,0:T(8,128)(2,1)S(1)}, bf16[2,128,2048]{1,2,0:T(8,128)(2,1)}, u32[]{:S(2)}) copy-start(bf16[2,128,2048]{1,2,0:T(8,128)(2,1)} %copy-done.4) | copy-start | bytes 3145732
  247.9 45.2 %copy-start.3 = (bf16[2,128,2048]{1,2,0:T(8,128)(2,1)S(1)}, bf16[2,128,2048]{1,2,0:T(8,128)(2,1)}, u32[]{:S(2)}) copy-start(bf16[2,128,2048]{1,2,0:T(8,128)(2,1)} %copy-done.2) | copy-start | bytes 3145732
  297.5 19.3 %copy-start.8 = (s32[1,6,2]{1,2,0:T(2,128)S(1)}, s32[1,6,2]{1,2,0:T(2,128)}, u32[]{:S(2)}) copy-start(s32[1,6,2]{1,2,0:T(2,128)} %param.8) | copy-start | bytes 148
  351.0 9.8 %copy-start.10 = (s32[1,6]{1,0:T(1,128)S(1)}, s32[1,6]{1,0:T(1,128)}, u32[]{:S(2)}) copy-start(s32[1,6]{1,0:T(1,128)} %param.9) | copy-start | bytes 76
  520.5 34.3 %copy-start.1 = (bf16[2,128,4096]{2,1,0:T(8,128)(2,1)S(1)}, bf16[2,128,4096]{2,1,0:T(8,128)(2,1)}, u32[]{:S(2)}) copy-start(bf16[2,128,4096]{2,1,0:T(8,128)(2,1)} %param.6) | copy-start | bytes 6291460
Sparse Core Ops, SparseCore 0:
  360.9 148.9 all-reduce.1
